TPU v7x, 32 devices: a whole 2x2x4 slice. The times are simulated.
32 devices in a mesh: rows: 8 (over z, y), cols: 4 (over x, core).
Axes of the slice: x: 2, y: 2, z: 4, core: 2. Of those that a mesh axis runs over, the one named last changes fastest.
Arguments:
- features: bfloat16 [4, 64, 640, 128], P(None, 'rows', 'cols'), may hold values from -60 to 60
- conv_first: bfloat16 [3, 3, 3, 128, 128], replicated, may hold values from -0.109375 to 0.109375
- first_reduce_kernel: bfloat16 [3, 3, 128, 256], replicated, may hold values from -0.1875 to 0.1875
- conv_second: bfloat16 [3, 3, 3, 256, 256], replicated, may hold values from -0.078125 to 0.078125
- second_reduce_kernel: bfloat16 [3, 3, 256, 512], replicated, may hold values from -0.125 to 0.125
- conv_last: bfloat16 [3, 3, 3, 512, 32], replicated, may hold values from -0.0546875 to 0.0546875
- gain_first: float32 [128], replicated, may hold values from 0.5 to 1.5
- shift_first: float32 [128], replicated, may hold values from -0.5 to 0.5
- gain_second: float32 [256], replicated, may hold values from 0.5 to 1.5
- shift_second: float32 [256], replicated, may hold values from -0.5 to 0.5
- gain_third: float32 [512], replicated, may hold values from 0.5 to 1.5
- shift_third: float32 [512], replicated, may hold values from -0.5 to 0.5
Outputs:
- moments: bfloat16 [4, 16, 160, 32], P(None, 'rows', 'cols')
All inputs are finite; a program needn't handle non-finite values.
Results may differ from a plain program's by a relative error of at most 0.01.
Values may be sent and summed in bfloat16 or wider, within the bound.
A program may use at most 64 MiB of HBM per device.

v0:
```python
import functools

import jax
import jax.numpy as jnp
from jax import lax
from jax.experimental import pallas as pl
from jax.experimental.pallas import tpu as pltpu
from jax.sharding import PartitionSpec as P

GROUPS = 32
EPSILON = 1e-06
LANES = 128
TILE = 8
MESH = pl.DeviceIdType.MESH
F32 = jnp.float32
BF16 = jnp.bfloat16

AROUND = [(-1, 0), (1, 0), (0, -1), (0, 1), (-1, -1), (-1, 1), (1, -1), (1, 1)]
BELOW = [(1, 0), (0, 1), (1, 1)]


def copies_needed(row_peers, col_peers):
    return 2 * len(AROUND) + len(AROUND) + 2 * len(BELOW) + 3 * (row_peers + col_peers - 2)


def packed_type(width):
    return BF16 if width % 16 == 0 else F32


class Net:
    def __init__(self, row_peers, col_peers, send, recv):
        self.row_peers, self.col_peers = row_peers, col_peers
        self.row, self.col = lax.axis_index("rows"), lax.axis_index("cols")
        self.send, self.recv = send, recv
        self.used = 0
        self.pending = []

    def exists(self, dr, dc):
        ok = None
        for place, peers, step in ((self.row, self.row_peers, dr), (self.col, self.col_peers, dc)):
            test = None
            if step < 0:
                test = place > 0
            elif step > 0:
                test = place < peers - 1
            if test is not None:
                ok = test if ok is None else jnp.logical_and(ok, test)
        return ok

    def barrier(self):
        sem = pltpu.get_barrier_semaphore()
        others = [(self.row, lax.rem(self.col + k, self.col_peers)) for k in range(1, self.col_peers)]
        others += [(lax.rem(self.row + k, self.row_peers), self.col) for k in range(1, self.row_peers)]
        others += [
            (
                lax.rem(self.row + dr + self.row_peers, self.row_peers),
                lax.rem(self.col + dc + self.col_peers, self.col_peers),
            )
            for dr, dc in AROUND
            if dr and dc
        ]
        for device in others:
            pl.semaphore_signal(sem, inc=1, device_id=device, device_id_type=MESH)
        pl.semaphore_wait(sem, len(others))

    def halo(self, dr, dc, src, dst):
        slot = self.used
        self.used += 1

        def copy():
            return pltpu.make_async_remote_copy(
                src_ref=src,
                dst_ref=dst,
                send_sem=self.send.at[slot],
                recv_sem=self.recv.at[slot],
                device_id=(self.row - dr, self.col - dc),
                device_id_type=MESH,
            )

        @pl.when(self.exists(-dr, -dc))
        def _():
            copy().start()

        def wait_send():
            @pl.when(self.exists(-dr, -dc))
            def _():
                copy().wait_send()

        return wait_send, lambda: copy().wait_recv()

    def all_sum(self, stat, partial, first, second):
        channels = stat.shape[1]
        total = self.axis_sum(stat, first, self.col_peers, lambda k: (self.row, lax.rem(self.col + k, self.col_peers)))
        partial[...] = total
        return self.axis_sum(partial, second, self.row_peers, lambda k: (lax.rem(self.row + k, self.row_peers), self.col))

    def axis_sum(self, src, slots, peers, device):
        copies = []
        for k in range(1, peers):
            copy = pltpu.make_async_remote_copy(
                src_ref=src,
                dst_ref=slots.at[k - 1],
                send_sem=self.send.at[self.used],
                recv_sem=self.recv.at[self.used],
                device_id=device(k),
                device_id_type=MESH,
            )
            self.used += 1
            copy.start()
            copies.append(copy)
            self.pending.append(copy.wait_send)
        total = src[...]
        for k, copy in enumerate(copies):
            copy.wait_recv()
            total = total + slots[k]
        return total


def group_sums(total):
    channels = total.shape[1]
    shift = (channels // GROUPS).bit_length() - 1
    row = lax.shift_right_logical(lax.broadcasted_iota(jnp.int32, (channels, channels), 0), shift)
    col = lax.shift_right_logical(lax.broadcasted_iota(jnp.int32, (channels, channels), 1), shift)
    same = jnp.where(row == col, 1.0, 0.0).astype(F32)
    return lax.dot_general(
        total, same, (((1,), (0,)), ((), ())),
        precision=lax.Precision.HIGHEST, preferred_element_type=F32,
    )


def norm_terms(total, members, gain):
    sums = group_sums(total) / members
    mean = sums[0:1]
    variance = jnp.maximum(sums[1:2] - mean * mean, 0.0)
    return mean, gain / jnp.sqrt(variance + EPSILON)


def silu_norm(values, mean, factor, shift):
    y = (values - mean) * factor + shift
    return y / (1.0 + jnp.exp(-y))


def clear_rim(buf):
    frames, high, wide, channels = buf.shape
    edge = jnp.zeros((TILE, channels), F32)
    line = jnp.zeros((wide, channels), F32)

    @pl.loop(0, frames)
    def _(t):
        buf[t, 0] = line
        buf[t, high - 1] = line
        for r in range(1, high - 1):
            buf[t, r, pl.ds(0, TILE), :] = edge
            buf[t, r, pl.ds(wide - TILE, TILE), :] = edge


def span(step, length, lead):
    if step < 0:
        return pl.ds(0, lead), pl.ds(length, lead)
    if step > 0:
        return pl.ds(lead + length, lead), pl.ds(lead, lead)
    return pl.ds(lead, length), pl.ds(lead, length)


def start_rim(net, buf, row_sources, row_slots):
    frames, high, wide, channels = buf.shape
    rows, cols = high - 2, wide - 2 * TILE
    parts = []
    for dr, dc in AROUND:
        if dc == 0:
            slot = 0 if dr < 0 else 1
            parts.append((dr, dc) + net.halo(dr, dc, row_sources[slot], row_slots.at[slot]))
            continue
        dst_cols, src_cols = span(dc, cols, TILE)
        dst_rows, src_rows = span(dr, rows, 1)
        parts.append(
            (dr, dc)
            + net.halo(
                dr, dc,
                buf.at[:, src_rows, src_cols, :],
                buf.at[:, dst_rows, dst_cols, :],
            )
        )
    return parts


def finish_rim(net, buf, row_slots, parts, change=None):
    frames, high, wide, channels = buf.shape
    rows, cols = high - 2, wide - 2 * TILE
    for dr, dc, wait_send, wait_recv in parts:
        net.pending.append(wait_send) if change is None else None

        @pl.when(net.exists(dr, dc))
        def _(dr=dr, dc=dc, wait_recv=wait_recv):
            wait_recv()
            if dc == 0:
                slot, place = (0, 0) if dr < 0 else (1, high - 1)

                @pl.loop(0, frames)
                def _(t):
                    value = row_slots[slot, t].astype(F32)
                    buf[t, place, pl.ds(TILE, cols), :] = value if change is None else change(value)
            elif change is not None:
                place_cols, _ = span(dc, cols, TILE)
                lines = range(1, high - 1) if dr == 0 else [0 if dr < 0 else high - 1]

                @pl.loop(0, frames)
                def _(t):
                    for r in lines:
                        buf[t, r, place_cols, :] = change(buf[t, r, place_cols, :])


def gather_taps(buf, taps):
    frames, high, wide, channels = buf.shape
    rows, cols = high - 2, wide - 2 * TILE

    @pl.loop(0, frames)
    def _(t):
        for r in range(high):
            for e in range(3):
                value = buf[t, r, pl.ds(TILE - 1 + e, cols), :].astype(taps.dtype)
                for b in range(3):
                    if 0 <= r - b < rows:
                        taps[t, pl.ds((r - b) * cols, cols), pl.ds((3 * b + e) * channels, channels)] = value


def gather_halved(act, taps):
    frames, high, blocks, wide, lanes = act.shape
    rows, cols = (high - 1) // 2, (wide - TILE) // 2
    channels = blocks * lanes

    @pl.loop(0, frames)
    def _(t):
        for r in range(rows):
            for b in range(3):
                for k in range(blocks):
                    for e in range(3):
                        value = act[t, 2 * r + b, k, pl.ds(e, cols, stride=2), :]
                        taps[t, pl.ds(r * cols, cols), pl.ds((3 * b + e) * channels + k * lanes, lanes)] = (
                            value.astype(taps.dtype)
                        )


def product(left, right):
    return jnp.dot(left.astype(BF16), right, preferred_element_type=F32)


def causal_product(taps, weights, pair, span_rows, emit):
    frames, places = taps.shape[:2]
    channels = weights.shape[2]

    def flat(first, last, places_at):
        value = taps[pl.ds(first, last - first), places_at, :]
        return value.reshape(-1, value.shape[2])

    def stretch(start):
        at = pl.ds(start, span_rows)
        at_frame = lambda value, t: value[t * span_rows : (t + 1) * span_rows]
        last = [None] * frames
        middle = [None] * frames
        oldest = [None] * frames
        if pair is not None:
            both = product(flat(0, frames - 1, at), pair[...])
            for t in range(frames - 1):
                middle[t] = at_frame(both, t)[:, :channels]
                last[t] = at_frame(both, t)[:, channels:]
            last[frames - 1] = product(flat(frames - 1, frames, at), weights[2])
        else:
            both = product(flat(0, frames, at), weights[2])
            last = [at_frame(both, t) for t in range(frames)]
            both = product(flat(0, frames - 1, at), weights[1])
            middle = [at_frame(both, t) for t in range(frames - 1)]
        both = product(flat(0, frames - 2, at), weights[0])
        oldest = [at_frame(both, t) for t in range(frames - 2)]
        emit(start, [
            oldest[max(t - 2, 0)] + middle[max(t - 1, 0)] + last[t] for t in range(frames)
        ])

    steps = places // span_rows
    if steps == 1:
        stretch(0)
    else:
        @pl.loop(0, steps)
        def _(step):
            stretch(pl.multiple_of(step * span_rows, span_rows))


def level(net, buf, taps, weights, pair, lines, act, halved, down, stats, members, gain, shift, ready):
    frames, high, blocks, wide, lanes = act.shape
    rows, cols = high - 1, wide - TILE
    stat, partial, first, second = stats
    gather_taps(buf, taps)
    stat[...] = jnp.zeros_like(stat)

    def emit(start, values):
        line = start // cols if isinstance(start, int) else lax.div(start, cols)
        for t, value in enumerate(values):
            stat[0:1] += jnp.sum(value, axis=0, keepdims=True)
            stat[1:2] += jnp.sum(value * value, axis=0, keepdims=True)
            for i in range(lines):
                for k in range(blocks):
                    act[t, line + i, k, pl.ds(0, cols), :] = value[
                        i * cols : (i + 1) * cols, k * lanes : (k + 1) * lanes
                    ]

    ready()
    causal_product(taps, weights, pair, lines * cols, emit)
    parts = []
    for dr, dc in BELOW:
        dst_rows, src_rows = (pl.ds(rows, 1), pl.ds(0, 1)) if dr else (pl.ds(0, rows), pl.ds(0, rows))
        dst_cols, src_cols = (pl.ds(cols, TILE), pl.ds(0, TILE)) if dc else (pl.ds(0, cols), pl.ds(0, cols))
        parts.append((dr, dc) + net.halo(
            dr, dc,
            act.at[:, src_rows, :, src_cols, :],
            act.at[:, dst_rows, :, dst_cols, :],
        ))
    total = net.all_sum(stat, partial, first, second)
    mean, factor = norm_terms(total, members, gain[...])
    bias = shift[...]

    def change(value, k):
        at = slice(k * lanes, (k + 1) * lanes)
        return silu_norm(value, mean[:, at], factor[:, at], bias[:, at])

    for _, _, wait_send, _ in parts:
        wait_send()

    @pl.loop(0, frames)
    def _(t):
        for r in range(rows):
            for k in range(blocks):
                act[t, r, k, pl.ds(0, cols), :] = change(act[t, r, k, pl.ds(0, cols), :], k)

    for dr, dc, _, wait_recv in parts:
        at = pl.ds(cols, TILE) if dc else pl.ds(0, cols)
        size = TILE if dc else cols
        places = [rows] if dr else list(range(rows))
        there = net.exists(dr, dc)

        @pl.when(there)
        def _(at=at, places=places, wait_recv=wait_recv):
            wait_recv()

            @pl.loop(0, frames)
            def _(t):
                for r in places:
                    for k in range(blocks):
                        act[t, r, k, at, :] = change(act[t, r, k, at, :], k)

        @pl.when(jnp.logical_not(there))
        def _(at=at, places=places, size=size):
            @pl.loop(0, frames)
            def _(t):
                for r in places:
                    for k in range(blocks):
                        act[t, r, k, at, :] = jnp.zeros((size, lanes), F32)

    gather_halved(act, halved)


def fill(buf, t, values, row_send):
    frames, high, wide, channels = buf.shape
    rows, cols = high - 2, wide - 2 * TILE
    for r in range(rows):
        value = values[r * cols : (r + 1) * cols].astype(BF16)
        buf[t, r + 1, pl.ds(TILE, cols), :] = value.astype(F32)
        if r == rows - 1:
            row_send[0, t] = value
        if r == 0:
            row_send[1, t] = value


def kernel(
    row_peers, col_peers,
    x, k1, d1, k2, d2, k3, g1, s1, g2, s2, g3, s3, out,
    xv, w1, pair1, v1, w2, v2, w3,
    buf1, taps1, act1, half1, slots1,
    buf2, taps2, act2, half2, sends2, slots2,
    buf3, taps3, sends3, slots3,
    stat1, part1, fa1, sa1, stat2, part2, fa2, sa2, stat3, part3, fa3, sa3,
    load, send, recv,
):
    net = Net(row_peers, col_peers, send, recv)
    frames, rows, cols, c1 = x.shape
    loads = [
        pltpu.make_async_copy(x, xv, load.at[0]),
        pltpu.make_async_copy(k1, w1, load.at[1]),
        pltpu.make_async_copy(k1.at[1], pair1.at[:, pl.ds(0, c1)], load.at[2]),
        pltpu.make_async_copy(k1.at[2], pair1.at[:, pl.ds(c1, c1)], load.at[3]),
        pltpu.make_async_copy(d1, v1, load.at[4]),
        pltpu.make_async_copy(k2, w2, load.at[5]),
        pltpu.make_async_copy(d2, v2, load.at[6]),
        pltpu.make_async_copy(k3, w3, load.at[7]),
    ]
    for copy in loads:
        copy.start()
    for buf in (buf1, buf2, buf3):
        clear_rim(buf)
    loads[0].wait()

    @pl.loop(0, frames)
    def _(t):
        for r in range(rows):
            buf1[t, r + 1, pl.ds(TILE, cols), :] = xv[t, r].astype(F32)

    net.barrier()
    places = float(frames * rows * cols * row_peers * col_peers)
    parts = start_rim(net, buf1, (x.at[:, rows - 1], x.at[:, 0]), slots1)
    finish_rim(net, buf1, slots1, parts)

    def ready1():
        for copy in loads[1:4]:
            copy.wait()

    level(
        net, buf1, taps1, w1, pair1, 2, act1, half1, v1, (stat1, part1, fa1, sa1),
        places * (c1 // GROUPS), g1, s1, ready1,
    )
    loads[4].wait()

    @pl.loop(0, frames)
    def _(t):
        fill(buf2, t, product(half1[t], v1[...]), sends2)

    parts = start_rim(net, buf2, (sends2.at[0], sends2.at[1]), slots2)
    finish_rim(net, buf2, slots2, parts)
    c2, c3 = v1.shape[1], v2.shape[1]
    level(
        net, buf2, taps2, w2, None, 2, act2, half2, v2, (stat2, part2, fa2, sa2),
        places / 4 * (c2 // GROUPS), g2, s2, loads[5].wait,
    )
    loads[6].wait()
    stat3[...] = jnp.zeros_like(stat3)

    @pl.loop(0, frames)
    def _(t):
        value = product(half2[t], v2[...])
        fill(buf3, t, value, sends3)
        value = value.astype(BF16).astype(F32)
        stat3[0:1] += jnp.sum(value, axis=0, keepdims=True)
        stat3[1:2] += jnp.sum(value * value, axis=0, keepdims=True)

    parts = start_rim(net, buf3, (sends3.at[0], sends3.at[1]), slots3)
    total = net.all_sum(stat3, part3, fa3, sa3)
    mean, factor = norm_terms(total, places / 16 * (c3 // GROUPS), g3[...])
    bias = s3[...]
    change = lambda value: silu_norm(value, mean, factor, bias)
    for _, _, wait_send, _ in parts:
        wait_send()
    rows3, cols3 = buf3.shape[1] - 2, buf3.shape[2] - 2 * TILE

    @pl.loop(0, frames)
    def _(t):
        for r in range(rows3):
            at = pl.ds(TILE, cols3)
            buf3[t, r + 1, at, :] = change(buf3[t, r + 1, at, :])

    finish_rim(net, buf3, slots3, parts, change)
    gather_taps(buf3, taps3)
    loads[7].wait()

    def emit(start, values):
        for t, value in enumerate(values):
            for r in range(rows3):
                out[t, r] = value[r * cols3 : (r + 1) * cols3].astype(BF16)

    causal_product(taps3, w3, None, rows3 * cols3, emit)
    for wait in net.pending:
        wait()


def shards(row_peers, col_peers, x, k1, d1, k2, d2, k3, g1, s1, g2, s2, g3, s3):
    frames, rows, cols, c1 = x.shape
    c2, c3, latent = d1.shape[3], d2.shape[3], k3.shape[4]
    channels = (c1, c2, c3)
    shapes = [(rows >> i, cols >> i) for i in range(3)]
    flat3 = lambda k: k.reshape(3, 9 * k.shape[3], k.shape[4])
    flat2 = lambda k: k.reshape(9 * k.shape[2], k.shape[3])
    weights = (flat3(k1), flat2(d1), flat3(k2), flat2(d2), flat3(k3))
    k1f, d1f, k2f, d2f, k3f = weights

    def padded(i):
        h, w = shapes[i]
        return pltpu.VMEM((frames, h + 2, w + 2 * TILE, channels[i]), F32)

    def taps(i):
        h, w = shapes[i]
        return pltpu.VMEM((frames, h * w, 9 * channels[i]), packed_type(w))

    def act(i):
        h, w = shapes[i]
        return pltpu.VMEM((frames, h + 1, channels[i] // LANES, w + TILE, LANES), F32)

    def half(i):
        h, w = shapes[i + 1]
        return pltpu.VMEM((frames, h * w, 9 * channels[i]), packed_type(w))

    def lines(i):
        return pltpu.VMEM((2, frames, shapes[i][1], channels[i]), BF16)

    def stats(i):
        c = channels[i]
        return [
            pltpu.VMEM((TILE, c), F32),
            pltpu.VMEM((TILE, c), F32),
            pltpu.VMEM((col_peers - 1, TILE, c), F32),
            pltpu.VMEM((row_peers - 1, TILE, c), F32),
        ]

    count = copies_needed(row_peers, col_peers)
    scratch = [
        pltpu.VMEM(x.shape, BF16),
        pltpu.VMEM(k1f.shape, BF16),
        pltpu.VMEM((k1f.shape[1], 2 * c1), BF16),
        pltpu.VMEM(d1f.shape, BF16),
        pltpu.VMEM(k2f.shape, BF16),
        pltpu.VMEM(d2f.shape, BF16),
        pltpu.VMEM(k3f.shape, BF16),
        padded(0), taps(0), act(0), half(0), lines(0),
        padded(1), taps(1), act(1), half(1), lines(1), lines(1),
        padded(2), taps(2), lines(2), lines(2),
        *stats(0), *stats(1), *stats(2),
        pltpu.SemaphoreType.DMA((8,)),
        pltpu.SemaphoreType.DMA((count,)),
        pltpu.SemaphoreType.DMA((count,)),
    ]
    anywhere = pl.BlockSpec(memory_space=pl.ANY)
    local = pl.BlockSpec(memory_space=pltpu.VMEM)
    wide = lambda v: v.reshape(1, -1)
    return pl.pallas_call(
        functools.partial(kernel, row_peers, col_peers),
        out_shape=jax.ShapeDtypeStruct((frames, *shapes[2], latent), BF16),
        in_specs=[anywhere] * 6 + [local] * 6,
        out_specs=local,
        scratch_shapes=scratch,
        compiler_params=pltpu.CompilerParams(
            collective_id=0, has_side_effects=True, vmem_limit_bytes=64000 * 1024
        ),
    )(x, *weights, *map(wide, (g1, s1, g2, s2, g3, s3)))


def solution(mesh):
    block = P(None, "rows", "cols", None)
    body = functools.partial(shards, mesh.shape["rows"], mesh.shape["cols"])
    return jax.shard_map(
        body, mesh=mesh, in_specs=(block,) + (P(),) * 11, out_specs=block, check_vma=False
    )
```

profile of v0, /device:TPU:9, one launch (start us, length us, event | category | flops | bytes accessed | tf_op | source)
XLA Modules:
  0.0 90.6 jit_solution(2845686296760414838)
XLA Ops:
  0.0 3.9 %copy.13 = bf16[3,3,3,512,32]{4,3,2,1,0:T(8,128)(2,1)} copy(bf16[3,3,3,512,32]{3,4,2,1,0:T(8,128)(2,1)} %param.17) | data formatting | bytes 1769472 | tf_op args[5]
  3.9 85.1 %shard_map.118 = bf16[4,2,40,32]{3,2,1,0:T(8,128)(2,1)} custom-call(bf16[4,8,160,128]{3,2,1,0:T(8,128)(2,1)} %x.1, bf16[3,1152,128]{2,1,0:T(8,128)(2,1)} %bitcast.14, bf16[1152,256]{1,0:T(8,128)(2,1)} %bitcast.15, bf16[3,2304,256]{2,1,0:T(8,128)(2,1)} %bitcast.12, bf16[2304,512]{1,0:T(8,128)(2,1)} %bitcast.13, bf16[3,4608,32]{2,1,0:T(8,128)(2,1)} %bitcast.11, ...), custom_call_target="tpu_custom_call" | custom-call | tf_op jit(solution)/shard_map/pallas_call | solution.py:530
  89.0 1.6 %copy.14 = bf16[4,2,40,32]{2,3,1,0:T(8,128)(2,1)} copy(bf16[4,2,40,32]{3,2,1,0:T(8,128)(2,1)} %shard_map.118) | data formatting | bytes 40960 | tf_op jit(solution)/shard_map/pallas_call | solution.py:530
where the time goes:
time: 91.2 us; the launch traced here: 90.6 us
  Pallas kernels  85.1 us (93%)
  local copies, waits for them, and re-layouts  5.5 us (6%)
    pallas_call x1, Pallas kernels, shards(): pl.pallas_call(functools.partial(kernel, row_peers, col_peers), out_shape...  85.1 us
    unnamed x1, local copies, waits for them, and re-layouts  3.89 us

commit v1 on v0

--- a/solution.py
+++ b/solution.py
@@ -10,6 +10,7 @@
 GROUPS = 32
 EPSILON = 1e-06
 LANES = 128
+EDGE = 16
 TILE = 8
 MESH = pl.DeviceIdType.MESH
 F32 = jnp.float32
@@ -47,7 +48,7 @@
                 ok = test if ok is None else jnp.logical_and(ok, test)
         return ok
 
-    def barrier(self):
+    def greet(self):
         sem = pltpu.get_barrier_semaphore()
         others = [(self.row, lax.rem(self.col + k, self.col_peers)) for k in range(1, self.col_peers)]
         others += [(lax.rem(self.row + k, self.row_peers), self.col) for k in range(1, self.row_peers)]
@@ -61,7 +62,7 @@
         ]
         for device in others:
             pl.semaphore_signal(sem, inc=1, device_id=device, device_id_type=MESH)
-        pl.semaphore_wait(sem, len(others))
+        return lambda: pl.semaphore_wait(sem, len(others))
 
     def halo(self, dr, dc, src, dst):
         slot = self.used
@@ -88,13 +89,15 @@
 
         return wait_send, lambda: copy().wait_recv()
 
-    def all_sum(self, stat, partial, first, second):
-        channels = stat.shape[1]
-        total = self.axis_sum(stat, first, self.col_peers, lambda k: (self.row, lax.rem(self.col + k, self.col_peers)))
-        partial[...] = total
-        return self.axis_sum(partial, second, self.row_peers, lambda k: (lax.rem(self.row + k, self.row_peers), self.col))
-
-    def axis_sum(self, src, slots, peers, device):
+    def all_sum(self, groups, stats, between=None, after=None):
+        own, partial, first, second = stats
+        own[...] = groups
+        along = lambda k: (self.row, lax.rem(self.col + k, self.col_peers))
+        across = lambda k: (lax.rem(self.row + k, self.row_peers), self.col)
+        partial[...] = self.axis_sum(own, first, self.col_peers, along, between)
+        return self.axis_sum(partial, second, self.row_peers, across, after)
+
+    def axis_sum(self, src, slots, peers, device, then):
         copies = []
         for k in range(1, peers):
             copy = pltpu.make_async_remote_copy(
@@ -109,6 +112,8 @@
             copy.start()
             copies.append(copy)
             self.pending.append(copy.wait_send)
+        if then is not None:
+            then()
         total = src[...]
         for k, copy in enumerate(copies):
             copy.wait_recv()
@@ -116,23 +121,33 @@
         return total
 
 
-def group_sums(total):
-    channels = total.shape[1]
-    shift = (channels // GROUPS).bit_length() - 1
-    row = lax.shift_right_logical(lax.broadcasted_iota(jnp.int32, (channels, channels), 0), shift)
-    col = lax.shift_right_logical(lax.broadcasted_iota(jnp.int32, (channels, channels), 1), shift)
-    same = jnp.where(row == col, 1.0, 0.0).astype(F32)
+def membership(channels, across):
+    shape = (channels, LANES) if across else (LANES, channels)
+    size = channels // GROUPS
+    channel = lax.broadcasted_iota(jnp.int32, shape, 0 if across else 1)
+    first = lax.broadcasted_iota(jnp.int32, shape, 1 if across else 0) * size
+    return jnp.where(jnp.logical_and(channel >= first, channel < first + size), 1.0, 0.0).astype(F32)
+
+
+def exact(left, right):
     return lax.dot_general(
-        total, same, (((1,), (0,)), ((), ())),
+        left, right, (((1,), (0,)), ((), ())),
         precision=lax.Precision.HIGHEST, preferred_element_type=F32,
     )
 
 
+def group_sums(stat):
+    return exact(stat[...], membership(stat.shape[1], True))[0:2]
+
+
 def norm_terms(total, members, gain):
-    sums = group_sums(total) / members
+    sums = total / members
     mean = sums[0:1]
     variance = jnp.maximum(sums[1:2] - mean * mean, 0.0)
-    return mean, gain / jnp.sqrt(variance + EPSILON)
+    inverse = 1.0 / jnp.sqrt(variance + EPSILON)
+    first = lax.broadcasted_iota(jnp.int32, (TILE, LANES), 0) == 0
+    spread = exact(jnp.where(first, mean, inverse), membership(gain.shape[1], False))
+    return spread[0:1], spread[1:2] * gain
 
 
 def silu_norm(values, mean, factor, shift):
@@ -210,18 +225,39 @@
                         buf[t, r, place_cols, :] = change(buf[t, r, place_cols, :])
 
 
-def gather_taps(buf, taps):
+def gather_taps(buf, taps, lines, spare):
     frames, high, wide, channels = buf.shape
     rows, cols = high - 2, wide - 2 * TILE
 
     @pl.loop(0, frames)
     def _(t):
-        for r in range(high):
+        for r in lines:
             for e in range(3):
-                value = buf[t, r, pl.ds(TILE - 1 + e, cols), :].astype(taps.dtype)
+                start = spare if e == 0 else 0
+                size = cols if e == 1 else cols - spare
+                value = buf[t, r, pl.ds(TILE - 1 + e + start, size), :].astype(taps.dtype)
                 for b in range(3):
                     if 0 <= r - b < rows:
-                        taps[t, pl.ds((r - b) * cols, cols), pl.ds((3 * b + e) * channels, channels)] = value
+                        put_taps(taps, t, r - b, start, size, 3 * b + e, value)
+
+
+def put_taps(taps, t, row, start, size, tap, value):
+    channels = value.shape[1]
+    taps[t, row, pl.ds(start, size), pl.ds(tap * channels, channels)] = value
+
+
+def patch_taps(buf, taps):
+    frames, high, wide, channels = buf.shape
+    rows, cols = high - 2, wide - 2 * TILE
+
+    @pl.loop(0, frames)
+    def _(t):
+        for r in range(1, high - 1):
+            for e, start in ((0, 0), (2, cols - EDGE)):
+                value = buf[t, r, pl.ds(TILE - 1 + e + start, EDGE), :].astype(taps.dtype)
+                for b in range(3):
+                    if 0 <= r - b < rows:
+                        put_taps(taps, t, r - b, start, EDGE, 3 * b + e, value)
 
 
 def gather_halved(act, taps):
@@ -245,76 +281,80 @@
     return jnp.dot(left.astype(BF16), right, preferred_element_type=F32)
 
 
-def causal_product(taps, weights, pair, span_rows, emit):
-    frames, places = taps.shape[:2]
+def causal_product(taps, weights, pair, block):
+    row, row_count, col, col_count = block
+    frames = taps.shape[0]
     channels = weights.shape[2]
-
-    def flat(first, last, places_at):
-        value = taps[pl.ds(first, last - first), places_at, :]
-        return value.reshape(-1, value.shape[2])
-
-    def stretch(start):
-        at = pl.ds(start, span_rows)
-        at_frame = lambda value, t: value[t * span_rows : (t + 1) * span_rows]
-        last = [None] * frames
-        middle = [None] * frames
-        oldest = [None] * frames
-        if pair is not None:
-            both = product(flat(0, frames - 1, at), pair[...])
-            for t in range(frames - 1):
-                middle[t] = at_frame(both, t)[:, :channels]
-                last[t] = at_frame(both, t)[:, channels:]
-            last[frames - 1] = product(flat(frames - 1, frames, at), weights[2])
-        else:
-            both = product(flat(0, frames, at), weights[2])
-            last = [at_frame(both, t) for t in range(frames)]
-            both = product(flat(0, frames - 1, at), weights[1])
-            middle = [at_frame(both, t) for t in range(frames - 1)]
-        both = product(flat(0, frames - 2, at), weights[0])
-        oldest = [at_frame(both, t) for t in range(frames - 2)]
-        emit(start, [
-            oldest[max(t - 2, 0)] + middle[max(t - 1, 0)] + last[t] for t in range(frames)
-        ])
-
-    steps = places // span_rows
-    if steps == 1:
-        stretch(0)
+    size = row_count * col_count
+
+    def flat(first, last):
+        value = taps[pl.ds(first, last - first), pl.ds(row, row_count), pl.ds(col, col_count), :]
+        return value.reshape(-1, value.shape[3])
+
+    def split(value):
+        return [value[t : t + size] for t in range(0, value.shape[0], size)]
+
+    if pair is not None:
+        both = split(product(flat(0, frames - 1), pair[...]))
+        middle = [value[:, :channels] for value in both]
+        last = [value[:, channels:] for value in both]
+        last += split(product(flat(frames - 1, frames), weights[2]))
     else:
-        @pl.loop(0, steps)
-        def _(step):
-            stretch(pl.multiple_of(step * span_rows, span_rows))
-
-
-def level(net, buf, taps, weights, pair, lines, act, halved, down, stats, members, gain, shift, ready):
+        last = split(product(flat(0, frames), weights[2]))
+        middle = split(product(flat(0, frames - 1), weights[1]))
+    oldest = split(product(flat(0, frames - 2), weights[0]))
+    return [oldest[max(t - 2, 0)] + middle[max(t - 1, 0)] + last[t] for t in range(frames)]
+
+
+def level(
+    net, buf, taps, weights, pair, blocks_of, act, halved, edges, stat, stats,
+    members, gain, shift, ready, rim_cols, rim_rows,
+):
     frames, high, blocks, wide, lanes = act.shape
     rows, cols = high - 1, wide - TILE
-    stat, partial, first, second = stats
-    gather_taps(buf, taps)
+    edge_send, edge_recv = edges
     stat[...] = jnp.zeros_like(stat)
 
-    def emit(start, values):
-        line = start // cols if isinstance(start, int) else lax.div(start, cols)
-        for t, value in enumerate(values):
+    def convolve(block):
+        row, row_count, col, col_count = block
+        for t, value in enumerate(causal_product(taps, weights, pair, block)):
             stat[0:1] += jnp.sum(value, axis=0, keepdims=True)
             stat[1:2] += jnp.sum(value * value, axis=0, keepdims=True)
-            for i in range(lines):
+            for i in range(row_count):
                 for k in range(blocks):
-                    act[t, line + i, k, pl.ds(0, cols), :] = value[
-                        i * cols : (i + 1) * cols, k * lanes : (k + 1) * lanes
+                    act[t, row + i, k, pl.ds(col, col_count), :] = value[
+                        i * col_count : (i + 1) * col_count, k * lanes : (k + 1) * lanes
                     ]
-
+            if row == 0:
+                edge_send[t] = value[:cols].astype(BF16)
+
+    early, middle, late = blocks_of
+    gather_taps(buf, taps, range(1, rows + 1), EDGE)
     ready()
-    causal_product(taps, weights, pair, lines * cols, emit)
+    for block in early:
+        convolve(block)
+    rim_cols()
+    patch_taps(buf, taps)
+    for block in middle:
+        convolve(block)
+    rim_rows()
+    gather_taps(buf, taps, (0, rows + 1), 0)
+    convolve((0, 1, 0, cols))
+    row_send, row_recv = net.halo(1, 0, edge_send, edge_recv)
+    for block in late:
+        convolve(block)
     parts = []
-    for dr, dc in BELOW:
-        dst_rows, src_rows = (pl.ds(rows, 1), pl.ds(0, 1)) if dr else (pl.ds(0, rows), pl.ds(0, rows))
-        dst_cols, src_cols = (pl.ds(cols, TILE), pl.ds(0, TILE)) if dc else (pl.ds(0, cols), pl.ds(0, cols))
-        parts.append((dr, dc) + net.halo(
-            dr, dc,
-            act.at[:, src_rows, :, src_cols, :],
-            act.at[:, dst_rows, :, dst_cols, :],
-        ))
-    total = net.all_sum(stat, partial, first, second)
+
+    def between():
+        for dr, dc in ((0, 1), (1, 1)):
+            dst_rows, src_rows = (pl.ds(rows, 1), pl.ds(0, 1)) if dr else (pl.ds(0, rows), pl.ds(0, rows))
+            parts.append((dr, dc) + net.halo(
+                dr, dc,
+                act.at[:, src_rows, :, pl.ds(0, TILE), :],
+                act.at[:, dst_rows, :, pl.ds(cols, TILE), :],
+            ))
+
+    total = net.all_sum(group_sums(stat), stats, between)
     mean, factor = norm_terms(total, members, gain[...])
     bias = shift[...]
 
@@ -322,6 +362,7 @@
         at = slice(k * lanes, (k + 1) * lanes)
         return silu_norm(value, mean[:, at], factor[:, at], bias[:, at])
 
+    net.pending.append(row_send)
     for _, _, wait_send, _ in parts:
         wait_send()
 
@@ -331,30 +372,37 @@
             for k in range(blocks):
                 act[t, r, k, pl.ds(0, cols), :] = change(act[t, r, k, pl.ds(0, cols), :], k)
 
-    for dr, dc, _, wait_recv in parts:
+    def border(dr, dc, finish):
         at = pl.ds(cols, TILE) if dc else pl.ds(0, cols)
         size = TILE if dc else cols
         places = [rows] if dr else list(range(rows))
         there = net.exists(dr, dc)
 
         @pl.when(there)
-        def _(at=at, places=places, wait_recv=wait_recv):
-            wait_recv()
+        def _():
+            finish()
 
             @pl.loop(0, frames)
             def _(t):
                 for r in places:
                     for k in range(blocks):
-                        act[t, r, k, at, :] = change(act[t, r, k, at, :], k)
+                        if dc:
+                            value = act[t, r, k, at, :]
+                        else:
+                            value = edge_recv[t, :, pl.ds(k * lanes, lanes)].astype(F32)
+                        act[t, r, k, at, :] = change(value, k)
 
         @pl.when(jnp.logical_not(there))
-        def _(at=at, places=places, size=size):
+        def _():
             @pl.loop(0, frames)
             def _(t):
                 for r in places:
                     for k in range(blocks):
                         act[t, r, k, at, :] = jnp.zeros((size, lanes), F32)
 
+    border(1, 0, row_recv)
+    for dr, dc, _, wait_recv in parts:
+        border(dr, dc, wait_recv)
     gather_halved(act, halved)
 
 
@@ -374,14 +422,15 @@
     row_peers, col_peers,
     x, k1, d1, k2, d2, k3, g1, s1, g2, s2, g3, s3, out,
     xv, w1, pair1, v1, w2, v2, w3,
-    buf1, taps1, act1, half1, slots1,
-    buf2, taps2, act2, half2, sends2, slots2,
+    buf1, taps1, act1, half1, slots1, edge1, edged1,
+    buf2, taps2, act2, half2, sends2, slots2, edge2, edged2,
     buf3, taps3, sends3, slots3,
-    stat1, part1, fa1, sa1, stat2, part2, fa2, sa2, stat3, part3, fa3, sa3,
+    stat1, own1, part1, fa1, sa1, stat2, own2, part2, fa2, sa2, stat3, own3, part3, fa3, sa3,
     load, send, recv,
 ):
     net = Net(row_peers, col_peers, send, recv)
     frames, rows, cols, c1 = x.shape
+    latent = k3.shape[2]
     loads = [
         pltpu.make_async_copy(x, xv, load.at[0]),
         pltpu.make_async_copy(k1, w1, load.at[1]),
@@ -390,12 +439,14 @@
         pltpu.make_async_copy(d1, v1, load.at[4]),
         pltpu.make_async_copy(k2, w2, load.at[5]),
         pltpu.make_async_copy(d2, v2, load.at[6]),
-        pltpu.make_async_copy(k3, w3, load.at[7]),
     ]
+    for a in range(3):
+        loads.append(pltpu.make_async_copy(k3.at[a], w3.at[:, pl.ds(a * latent, latent), :], load.at[7 + a]))
     for copy in loads:
         copy.start()
     for buf in (buf1, buf2, buf3):
         clear_rim(buf)
+    arrive = net.greet()
     loads[0].wait()
 
     @pl.loop(0, frames)
@@ -403,18 +454,27 @@
         for r in range(rows):
             buf1[t, r + 1, pl.ds(TILE, cols), :] = xv[t, r].astype(F32)
 
-    net.barrier()
     places = float(frames * rows * cols * row_peers * col_peers)
-    parts = start_rim(net, buf1, (x.at[:, rows - 1], x.at[:, 0]), slots1)
-    finish_rim(net, buf1, slots1, parts)
+    held = []
+    beside = lambda parts: [part for part in parts if part[0] == 0]
+    beyond = lambda parts: [part for part in parts if part[0] != 0]
+
+    def rim_cols1():
+        arrive()
+        held.extend(start_rim(net, buf1, (x.at[:, rows - 1], x.at[:, 0]), slots1))
+        finish_rim(net, buf1, slots1, beside(held))
 
     def ready1():
         for copy in loads[1:4]:
             copy.wait()
 
+    within = [(1, rows - 2, EDGE, cols - 2 * EDGE)]
+    strips = [(1, rows - 2, 0, EDGE), (1, rows - 2, cols - EDGE, EDGE)]
     level(
-        net, buf1, taps1, w1, pair1, 2, act1, half1, v1, (stat1, part1, fa1, sa1),
+        net, buf1, taps1, w1, pair1, (within, strips, [(rows - 1, 1, 0, cols)]),
+        act1, half1, (edge1, edged1), stat1, (own1, part1, fa1, sa1),
         places * (c1 // GROUPS), g1, s1, ready1,
+        rim_cols1, lambda: finish_rim(net, buf1, slots1, beyond(held)),
     )
     loads[4].wait()
 
@@ -423,11 +483,15 @@
         fill(buf2, t, product(half1[t], v1[...]), sends2)
 
     parts = start_rim(net, buf2, (sends2.at[0], sends2.at[1]), slots2)
-    finish_rim(net, buf2, slots2, parts)
     c2, c3 = v1.shape[1], v2.shape[1]
+    rows2, cols2 = buf2.shape[1] - 2, buf2.shape[2] - 2 * TILE
     level(
-        net, buf2, taps2, w2, None, 2, act2, half2, v2, (stat2, part2, fa2, sa2),
+        net, buf2, taps2, w2, None,
+        ([], [(1, rows2 - 2, 0, cols2)], [(rows2 - 1, 1, 0, cols2)]),
+        act2, half2, (edge2, edged2), stat2, (own2, part2, fa2, sa2),
         places / 4 * (c2 // GROUPS), g2, s2, loads[5].wait,
+        lambda: finish_rim(net, buf2, slots2, beside(parts)),
+        lambda: finish_rim(net, buf2, slots2, beyond(parts)),
     )
     loads[6].wait()
     stat3[...] = jnp.zeros_like(stat3)
@@ -440,13 +504,16 @@
         stat3[0:1] += jnp.sum(value, axis=0, keepdims=True)
         stat3[1:2] += jnp.sum(value * value, axis=0, keepdims=True)
 
-    parts = start_rim(net, buf3, (sends3.at[0], sends3.at[1]), slots3)
-    total = net.all_sum(stat3, part3, fa3, sa3)
+    rims = []
+    total = net.all_sum(
+        group_sums(stat3), (own3, part3, fa3, sa3), None,
+        lambda: rims.extend(start_rim(net, buf3, (sends3.at[0], sends3.at[1]), slots3)),
+    )
     mean, factor = norm_terms(total, places / 16 * (c3 // GROUPS), g3[...])
     bias = s3[...]
     change = lambda value: silu_norm(value, mean, factor, bias)
-    for _, _, wait_send, _ in parts:
-        wait_send()
+    for dr, dc, wait_send, _ in rims:
+        net.pending.append(wait_send) if dc == 0 else wait_send()
     rows3, cols3 = buf3.shape[1] - 2, buf3.shape[2] - 2 * TILE
 
     @pl.loop(0, frames)
@@ -455,16 +522,33 @@
             at = pl.ds(TILE, cols3)
             buf3[t, r + 1, at, :] = change(buf3[t, r + 1, at, :])
 
-    finish_rim(net, buf3, slots3, parts, change)
-    gather_taps(buf3, taps3)
-    loads[7].wait()
-
-    def emit(start, values):
-        for t, value in enumerate(values):
-            for r in range(rows3):
-                out[t, r] = value[r * cols3 : (r + 1) * cols3].astype(BF16)
-
-    causal_product(taps3, w3, None, rows3 * cols3, emit)
+    finish_rim(net, buf3, slots3, rims, change)
+
+    @pl.loop(0, frames)
+    def _(t):
+        for r in range(rows3 + 2):
+            for e in range(3):
+                value = buf3[t, r, pl.ds(TILE - 1 + e, cols3), :]
+                for b in range(3):
+                    if 0 <= r - b < rows3:
+                        taps3[t, pl.ds((r - b) * cols3, cols3), pl.ds((3 * b + e) * c3, c3)] = value
+
+    for copy in loads[7:]:
+        copy.wait()
+    total = None
+    for tap in range(9):
+        left = taps3[:, :, pl.ds(tap * c3, c3)].reshape(-1, c3).astype(BF16)
+        term = lax.dot_general(left, w3[tap], (((1,), (1,)), ((), ())), preferred_element_type=F32)
+        total = term if total is None else total + term
+    size = rows3 * cols3
+    ages = [
+        [total[t * size : (t + 1) * size, a * latent : (a + 1) * latent] for t in range(frames)]
+        for a in range(3)
+    ]
+    for t in range(frames):
+        value = ages[0][max(t - 2, 0)] + ages[1][max(t - 1, 0)] + ages[2][t]
+        for r in range(rows3):
+            out[t, r] = value[r * cols3 : (r + 1) * cols3].astype(BF16)
     for wait in net.pending:
         wait()
 
@@ -476,8 +560,9 @@
     shapes = [(rows >> i, cols >> i) for i in range(3)]
     flat3 = lambda k: k.reshape(3, 9 * k.shape[3], k.shape[4])
     flat2 = lambda k: k.reshape(9 * k.shape[2], k.shape[3])
-    weights = (flat3(k1), flat2(d1), flat3(k2), flat2(d2), flat3(k3))
-    k1f, d1f, k2f, d2f, k3f = weights
+    k3 = jnp.swapaxes(k3, 3, 4).reshape(3, 9, latent, c3)
+    weights = (flat3(k1), flat2(d1), flat3(k2), flat2(d2), k3)
+    k1f, d1f, k2f, d2f, _ = weights
 
     def padded(i):
         h, w = shapes[i]
@@ -485,7 +570,14 @@
 
     def taps(i):
         h, w = shapes[i]
-        return pltpu.VMEM((frames, h * w, 9 * channels[i]), packed_type(w))
+        return pltpu.VMEM((frames, h, w, 9 * channels[i]), BF16)
+
+    def last_taps():
+        h, w = shapes[2]
+        return pltpu.VMEM((frames, h * w, 9 * channels[2]), F32)
+
+    def edge(i):
+        return pltpu.VMEM((frames, shapes[i][1], channels[i]), BF16)
 
     def act(i):
         h, w = shapes[i]
@@ -502,9 +594,10 @@
         c = channels[i]
         return [
             pltpu.VMEM((TILE, c), F32),
-            pltpu.VMEM((TILE, c), F32),
-            pltpu.VMEM((col_peers - 1, TILE, c), F32),
-            pltpu.VMEM((row_peers - 1, TILE, c), F32),
+            pltpu.VMEM((2, LANES), F32),
+            pltpu.VMEM((2, LANES), F32),
+            pltpu.VMEM((col_peers - 1, 2, LANES), F32),
+            pltpu.VMEM((row_peers - 1, 2, LANES), F32),
         ]
 
     count = copies_needed(row_peers, col_peers)
@@ -515,12 +608,12 @@
         pltpu.VMEM(d1f.shape, BF16),
         pltpu.VMEM(k2f.shape, BF16),
         pltpu.VMEM(d2f.shape, BF16),
-        pltpu.VMEM(k3f.shape, BF16),
-        padded(0), taps(0), act(0), half(0), lines(0),
-        padded(1), taps(1), act(1), half(1), lines(1), lines(1),
-        padded(2), taps(2), lines(2), lines(2),
+        pltpu.VMEM((9, 3 * latent, c3), BF16),
+        padded(0), taps(0), act(0), half(0), lines(0), edge(0), edge(0),
+        padded(1), taps(1), act(1), half(1), lines(1), lines(1), edge(1), edge(1),
+        padded(2), last_taps(), lines(2), lines(2),
         *stats(0), *stats(1), *stats(2),
-        pltpu.SemaphoreType.DMA((8,)),
+        pltpu.SemaphoreType.DMA((10,)),
         pltpu.SemaphoreType.DMA((count,)),
         pltpu.SemaphoreType.DMA((count,)),
     ]

time: 91.2 us -> 75.4 us (0.83)
  Pallas kernels: 85.1 us -> 72.6 us
  local copies, waits for them, and re-layouts: 5.5 us -> 1.61 us
    pallas_call x1, Pallas kernels: 85.1 us -> 72.6 us  [shards(): pl.pallas_call(functools.partial(kernel, row_peers, col_peers), out_shape...]
    unnamed x1 -> x0, local copies, waits for them, and re-layouts: 3.89 us -> none
where the time goes in v1:
time: 75.4 us; the launch traced here: 74.2 us
  Pallas kernels  72.6 us (96%)
  local copies, waits for them, and re-layouts  1.61 us (2%)
    pallas_call x1, Pallas kernels, shards(): pl.pallas_call(functools.partial(kernel, row_peers, col_peers), out_shape...  72.6 us
    pallas_call x1, local copies, waits for them, and re-layouts, shards(): pl.pallas_call(functools.partial(kernel, row_peers, col_peers), out_shape...  1.61 us

profile of v1, /device:TPU:9, one launch (start us, length us, event | category | flops | bytes accessed | tf_op | source)
XLA Modules:
  0.0 74.2 jit_solution(12302124458227871516)
XLA Ops:
  0.0 72.6 %shard_map.118 = bf16[4,2,40,32]{3,2,1,0:T(8,128)(2,1)} custom-call(bf16[4,8,160,128]{3,2,1,0:T(8,128)(2,1)} %x.1, bf16[3,1152,128]{2,1,0:T(8,128)(2,1)} %bitcast.15, bf16[1152,256]{1,0:T(8,128)(2,1)} %bitcast.17, bf16[3,2304,256]{2,1,0:T(8,128)(2,1)} %bitcast.13, bf16[2304,512]{1,0:T(8,128)(2,1)} %bitcast.14, bf16[3,9,32,512]{3,2,1,0:T(8,128)(2,1)} %bitcast.16, ...), custom_call_target="tpu_custom_call" | custom-call | tf_op jit(solution)/shard_map/pallas_call | solution.py:623
  72.6 1.6 %copy.13 = bf16[4,2,40,32]{2,3,1,0:T(8,128)(2,1)} copy(bf16[4,2,40,32]{3,2,1,0:T(8,128)(2,1)} %shard_map.118) | data formatting | bytes 40960 | tf_op jit(solution)/shard_map/pallas_call | solution.py:623

commit v2 on v1

--- a/solution.py
+++ b/solution.py
@@ -21,7 +21,7 @@
 
 
 def copies_needed(row_peers, col_peers):
-    return 2 * len(AROUND) + len(AROUND) + 2 * len(BELOW) + 3 * (row_peers + col_peers - 2)
+    return 2 * len(AROUND) + len(AROUND) + 2 * (len(BELOW) + 1) + 3 * (row_peers + col_peers - 2)
 
 
 def packed_type(width):
@@ -312,7 +312,7 @@
 ):
     frames, high, blocks, wide, lanes = act.shape
     rows, cols = high - 1, wide - TILE
-    edge_send, edge_recv = edges
+    edge_send, edge_recv, center_send, center_recv = edges
     stat[...] = jnp.zeros_like(stat)
 
     def convolve(block):
@@ -325,8 +325,6 @@
                     act[t, row + i, k, pl.ds(col, col_count), :] = value[
                         i * col_count : (i + 1) * col_count, k * lanes : (k + 1) * lanes
                     ]
-            if row == 0:
-                edge_send[t] = value[:cols].astype(BF16)
 
     early, middle, late = blocks_of
     gather_taps(buf, taps, range(1, rows + 1), EDGE)
@@ -339,13 +337,21 @@
         convolve(block)
     rim_rows()
     gather_taps(buf, taps, (0, rows + 1), 0)
-    convolve((0, 1, 0, cols))
-    row_send, row_recv = net.halo(1, 0, edge_send, edge_recv)
     for block in late:
         convolve(block)
-    parts = []
+    parts, lines = [], []
 
     def between():
+        center = stat[0:1] / float(frames * rows * cols)
+        center_send[...] = jnp.broadcast_to(center, center_send.shape)
+
+        @pl.loop(0, frames)
+        def _(t):
+            for k in range(blocks):
+                at = slice(k * lanes, (k + 1) * lanes)
+                value = act[t, 0, k, pl.ds(0, cols), :] - center[:, at]
+                edge_send[t, :, pl.ds(k * lanes, lanes)] = value.astype(BF16)
+
         for dr, dc in ((0, 1), (1, 1)):
             dst_rows, src_rows = (pl.ds(rows, 1), pl.ds(0, 1)) if dr else (pl.ds(0, rows), pl.ds(0, rows))
             parts.append((dr, dc) + net.halo(
@@ -354,7 +360,11 @@
                 act.at[:, dst_rows, :, pl.ds(cols, TILE), :],
             ))
 
-    total = net.all_sum(group_sums(stat), stats, between)
+    def after():
+        lines.append(net.halo(1, 0, center_send, center_recv))
+        lines.append(net.halo(1, 0, edge_send, edge_recv))
+
+    total = net.all_sum(group_sums(stat), stats, between, after)
     mean, factor = norm_terms(total, members, gain[...])
     bias = shift[...]
 
@@ -362,7 +372,7 @@
         at = slice(k * lanes, (k + 1) * lanes)
         return silu_norm(value, mean[:, at], factor[:, at], bias[:, at])
 
-    net.pending.append(row_send)
+    net.pending.extend(wait_send for wait_send, _ in lines)
     for _, _, wait_send, _ in parts:
         wait_send()
 
@@ -390,6 +400,7 @@
                             value = act[t, r, k, at, :]
                         else:
                             value = edge_recv[t, :, pl.ds(k * lanes, lanes)].astype(F32)
+                            value = value + center_recv[0:1, pl.ds(k * lanes, lanes)]
                         act[t, r, k, at, :] = change(value, k)
 
         @pl.when(jnp.logical_not(there))
@@ -400,7 +411,7 @@
                     for k in range(blocks):
                         act[t, r, k, at, :] = jnp.zeros((size, lanes), F32)
 
-    border(1, 0, row_recv)
+    border(1, 0, lambda: [wait_recv() for _, wait_recv in lines])
     for dr, dc, _, wait_recv in parts:
         border(dr, dc, wait_recv)
     gather_halved(act, halved)
@@ -422,8 +433,8 @@
     row_peers, col_peers,
     x, k1, d1, k2, d2, k3, g1, s1, g2, s2, g3, s3, out,
     xv, w1, pair1, v1, w2, v2, w3,
-    buf1, taps1, act1, half1, slots1, edge1, edged1,
-    buf2, taps2, act2, half2, sends2, slots2, edge2, edged2,
+    buf1, taps1, act1, half1, slots1, edge1, edged1, center1, centered1,
+    buf2, taps2, act2, half2, sends2, slots2, edge2, edged2, center2, centered2,
     buf3, taps3, sends3, slots3,
     stat1, own1, part1, fa1, sa1, stat2, own2, part2, fa2, sa2, stat3, own3, part3, fa3, sa3,
     load, send, recv,
@@ -471,8 +482,8 @@
     within = [(1, rows - 2, EDGE, cols - 2 * EDGE)]
     strips = [(1, rows - 2, 0, EDGE), (1, rows - 2, cols - EDGE, EDGE)]
     level(
-        net, buf1, taps1, w1, pair1, (within, strips, [(rows - 1, 1, 0, cols)]),
-        act1, half1, (edge1, edged1), stat1, (own1, part1, fa1, sa1),
+        net, buf1, taps1, w1, pair1, (within, strips, [(0, 1, 0, cols), (rows - 1, 1, 0, cols)]),
+        act1, half1, (edge1, edged1, center1, centered1), stat1, (own1, part1, fa1, sa1),
         places * (c1 // GROUPS), g1, s1, ready1,
         rim_cols1, lambda: finish_rim(net, buf1, slots1, beyond(held)),
     )
@@ -487,8 +498,8 @@
     rows2, cols2 = buf2.shape[1] - 2, buf2.shape[2] - 2 * TILE
     level(
         net, buf2, taps2, w2, None,
-        ([], [(1, rows2 - 2, 0, cols2)], [(rows2 - 1, 1, 0, cols2)]),
-        act2, half2, (edge2, edged2), stat2, (own2, part2, fa2, sa2),
+        ([], [], [(0, rows2, 0, cols2)]),
+        act2, half2, (edge2, edged2, center2, centered2), stat2, (own2, part2, fa2, sa2),
         places / 4 * (c2 // GROUPS), g2, s2, loads[5].wait,
         lambda: finish_rim(net, buf2, slots2, beside(parts)),
         lambda: finish_rim(net, buf2, slots2, beyond(parts)),
@@ -504,11 +515,8 @@
         stat3[0:1] += jnp.sum(value, axis=0, keepdims=True)
         stat3[1:2] += jnp.sum(value * value, axis=0, keepdims=True)
 
-    rims = []
-    total = net.all_sum(
-        group_sums(stat3), (own3, part3, fa3, sa3), None,
-        lambda: rims.extend(start_rim(net, buf3, (sends3.at[0], sends3.at[1]), slots3)),
-    )
+    rims = start_rim(net, buf3, (sends3.at[0], sends3.at[1]), slots3)
+    total = net.all_sum(group_sums(stat3), (own3, part3, fa3, sa3))
     mean, factor = norm_terms(total, places / 16 * (c3 // GROUPS), g3[...])
     bias = s3[...]
     change = lambda value: silu_norm(value, mean, factor, bias)
@@ -576,6 +584,9 @@
         h, w = shapes[2]
         return pltpu.VMEM((frames, h * w, 9 * channels[2]), F32)
 
+    def center(i):
+        return pltpu.VMEM((TILE, channels[i]), F32)
+
     def edge(i):
         return pltpu.VMEM((frames, shapes[i][1], channels[i]), BF16)
 
@@ -609,8 +620,8 @@
         pltpu.VMEM(k2f.shape, BF16),
         pltpu.VMEM(d2f.shape, BF16),
         pltpu.VMEM((9, 3 * latent, c3), BF16),
-        padded(0), taps(0), act(0), half(0), lines(0), edge(0), edge(0),
-        padded(1), taps(1), act(1), half(1), lines(1), lines(1), edge(1), edge(1),
+        padded(0), taps(0), act(0), half(0), lines(0), edge(0), edge(0), center(0), center(0),
+        padded(1), taps(1), act(1), half(1), lines(1), lines(1), edge(1), edge(1), center(1), center(1),
         padded(2), last_taps(), lines(2), lines(2),
         *stats(0), *stats(1), *stats(2),
         pltpu.SemaphoreType.DMA((10,)),

time: 75.4 us -> 76.4 us (1.013); the launches traced: 74.2 us -> 76.2 us
  Pallas kernels: 72.6 us -> 74.6 us
    pallas_call x1, Pallas kernels: 72.6 us -> 74.6 us  [shards(): pl.pallas_call(functools.partial(kernel, row_peers, col_peers), out_shape...]
where the time goes in v2:
time: 76.4 us; the launch traced here: 76.2 us
  Pallas kernels  74.6 us (98%)
  local copies, waits for them, and re-layouts  1.61 us (2%)
    pallas_call x1, Pallas kernels, shards(): pl.pallas_call(functools.partial(kernel, row_peers, col_peers), out_shape...  74.6 us
    pallas_call x1, local copies, waits for them, and re-layouts, shards(): pl.pallas_call(functools.partial(kernel, row_peers, col_peers), out_shape...  1.61 us

profile of v2, /device:TPU:9, one launch (start us, length us, event | category | flops | bytes accessed | tf_op | source)
XLA Modules:
  0.0 76.2 jit_solution(5311216411256344725)
XLA Ops:
  0.0 74.6 %shard_map.118 = bf16[4,2,40,32]{3,2,1,0:T(8,128)(2,1)} custom-call(bf16[4,8,160,128]{3,2,1,0:T(8,128)(2,1)} %x.1, bf16[3,1152,128]{2,1,0:T(8,128)(2,1)} %bitcast.15, bf16[1152,256]{1,0:T(8,128)(2,1)} %bitcast.17, bf16[3,2304,256]{2,1,0:T(8,128)(2,1)} %bitcast.13, bf16[2304,512]{1,0:T(8,128)(2,1)} %bitcast.14, bf16[3,9,32,512]{3,2,1,0:T(8,128)(2,1)} %bitcast.16, ...), custom_call_target="tpu_custom_call" | custom-call | tf_op jit(solution)/shard_map/pallas_call | solution.py:634
  74.6 1.6 %copy.13 = bf16[4,2,40,32]{2,3,1,0:T(8,128)(2,1)} copy(bf16[4,2,40,32]{3,2,1,0:T(8,128)(2,1)} %shard_map.118) | data formatting | bytes 40960 | tf_op jit(solution)/shard_map/pallas_call | solution.py:634
